TPU v7x, 256 devices: a whole 4x4x8 slice. The times are simulated.
256 devices in a mesh: dp: 2 (over core), ctx: 32 (over y, z), grp: 4 (over x).
Axes of the slice: x: 4, y: 4, z: 8, core: 2. Of those that a mesh axis runs over, the one named last changes fastest.
Arguments:
- projected: bfloat16 [4, 8192, 3, 4096], P('dp', 'ctx', None, 'grp'), may hold values from -6 to 6
- short_w: float32 [3, 3, 4096], P(None, None, 'grp'), may hold values from -2.5 to 2.5
- medium_h: bfloat16 [256, 128], P('grp'), may hold values from -3 to 3
- out_w: bfloat16 [4096, 4096], P('ctx', 'grp'), may hold values from -0.09375 to 0.09375
- grad_out: bfloat16 [4, 8192, 4096], P('dp', 'ctx', 'grp'), may hold values from -6 to 6
Outputs:
- block_out: bfloat16 [4, 8192, 4096], P('dp', 'ctx', 'grp')
- grad_projected: bfloat16 [4, 8192, 3, 4096], P('dp', 'ctx', None, 'grp')
- filter_grad: float32 [256, 128], P('grp')
- short_grad: float32 [3, 3, 4096], P(None, None, 'grp')
All inputs are finite; a program needn't handle non-finite values.
Results may differ from a plain program's by a relative error of at most 0.0064.
Values may be sent and summed in bfloat16 or wider, within the bound.
A program may use at most 128 MiB of HBM per device.

v0:
```python
import math
import jax
import jax.numpy as jnp
from jax import lax
from jax.sharding import PartitionSpec as P


def from_behind(block, axis, distance):
    devices = range(lax.axis_size(axis))
    route = [(i - distance, i) for i in devices if i - distance in devices]
    return lax.ppermute(block, axis, route)


def windows(padded, block_rows, reach):
    seqs_here = padded.shape[0]
    block_count = (padded.shape[1] - reach) // block_rows
    extended = jnp.pad(padded, ((0, 0), (0, block_rows - reach), (0, 0), (0, 0)))
    leading = extended[:, : block_count * block_rows].reshape(
        seqs_here, block_count, block_rows, padded.shape[2], padded.shape[3]
    )
    second = extended[:, block_rows:].reshape(
        seqs_here, block_count, block_rows, padded.shape[2], padded.shape[3]
    )[:, :, :reach]
    return jnp.concatenate([leading, second], axis=2)


def banded(filters, block_rows):
    groups_here = filters.shape[0]
    tap_count = filters.shape[1]
    line_width = block_rows + tap_count
    padded_line = jnp.concatenate(
        [filters, jnp.zeros((groups_here, block_rows), filters.dtype)], axis=1
    )
    tiled = jnp.broadcast_to(
        padded_line[:, None, :], (groups_here, block_rows, line_width)
    ).reshape(groups_here, block_rows * line_width)
    return tiled[:, : block_rows * (line_width - 1)].reshape(
        groups_here, block_rows, line_width - 1
    )


def band_conv(turned, matrix, block_rows):
    reach = matrix.shape[2] - block_rows
    windowed = windows(turned, block_rows, reach)
    result = jnp.einsum("gtj,sbjcg->sbtcg", matrix, windowed, preferred_element_type=jnp.float32)
    result = jnp.swapaxes(result, 3, 4)
    return result.reshape(
        turned.shape[0], turned.shape[1] - reach, turned.shape[2] * turned.shape[3]
    )


def lag_sums(grad_blocks, windowed, tap_count):
    products = jnp.einsum(
        "sbtcg,sbjcg->gtj", grad_blocks, windowed, preferred_element_type=jnp.float32
    )
    groups_here = products.shape[0]
    block_rows = products.shape[1]
    line_width = products.shape[2]
    flat_rows = jnp.pad(
        products.reshape(groups_here, block_rows * line_width), ((0, 0), (0, block_rows))
    )
    skewed = flat_rows.reshape(groups_here, block_rows, line_width + 1)[:, :, :tap_count]
    return jnp.sum(skewed, axis=1)[:, ::-1]


def featurize(padded, weights):
    short_reach = weights.shape[1] - 1
    row_count = padded.shape[1] - short_reach
    total = None
    for offset in range(weights.shape[1]):
        start = short_reach - offset
        term = weights[:, offset, :] * padded[:, start : start + row_count]
        total = term if total is None else total + term
    return total


def adjoint(padded, weights):
    short_reach = weights.shape[1] - 1
    row_count = padded.shape[1] - short_reach
    total = None
    for offset in range(weights.shape[1]):
        term = weights[:, offset, :] * padded[:, offset : offset + row_count]
        total = term if total is None else total + term
    return total


def short_sums(feature_grad, padded, short_taps):
    row_count = feature_grad.shape[1]
    short_reach = short_taps - 1
    terms = []
    for offset in range(short_taps):
        start = short_reach - offset
        terms.append(jnp.sum(feature_grad * padded[:, start : start + row_count], axis=(0, 1)))
    return jnp.stack(terms, axis=1)


def shards(projected, short_w, medium_h, out_w, grad_out):
    seq_local = projected.shape[0]
    row_count = projected.shape[1]
    chan_local = projected.shape[3]
    tap_count = medium_h.shape[1]
    reach = tap_count - 1
    short_taps = short_w.shape[1]
    short_reach = short_taps - 1
    group_local = medium_h.shape[0]
    group_size = chan_local // group_local
    block_rows = math.gcd(row_count, 128)
    front_rows = from_behind(projected[:, row_count - short_reach :], "ctx", 1)
    padded_input = jnp.concatenate([front_rows, projected], axis=1)
    features = featurize(padded_input.astype(jnp.float32), short_w)
    product = (features[:, :, 1] * features[:, :, 2]).astype(jnp.bfloat16)
    product_front = from_behind(product[:, row_count - reach :], "ctx", 1)
    product_pad = jnp.concatenate([product_front, product], axis=1)
    query = features[:, :, 0]
    keys = features[:, :, 1]
    values = features[:, :, 2]
    product_turned = jnp.swapaxes(
        product_pad.reshape(seq_local, row_count + reach, group_local, group_size), 2, 3
    )
    mixed = band_conv(product_turned, banded(medium_h[:, ::-1], block_rows), block_rows)
    gated = (query * mixed).astype(jnp.bfloat16)
    whole_gated = lax.all_gather(gated, "grp", axis=2, tiled=True)
    flat_gated = whole_gated.reshape(seq_local * row_count, whole_gated.shape[2])
    flat_cotangent = grad_out.reshape(seq_local * row_count, chan_local)
    projected_out = jnp.dot(
        flat_gated,
        lax.all_gather(out_w, "ctx", axis=0, tiled=True),
        preferred_element_type=jnp.float32,
    )
    block_out = projected_out.astype(jnp.bfloat16).reshape(seq_local, row_count, chan_local)
    input_part = lax.dot_general(
        flat_cotangent,
        lax.all_gather(out_w, "ctx", axis=0, tiled=True),
        (((1,), (1,)), ((), ())),
        preferred_element_type=jnp.float32,
    )
    summed = lax.psum_scatter(input_part, "grp", scatter_dimension=1, tiled=True)
    gated_grad = (
        lax.optimization_barrier(summed.astype(jnp.bfloat16))
        .astype(jnp.float32)
        .reshape(seq_local, row_count, chan_local)
    )
    query_grad = gated_grad * mixed
    mix_grad = (gated_grad * query).astype(jnp.bfloat16)
    mix_back = from_behind(mix_grad[:, :reach], "ctx", -1)
    mix_turned = jnp.swapaxes(
        jnp.concatenate([mix_grad, mix_back], axis=1).reshape(
            seq_local, row_count + reach, group_local, group_size
        ),
        2,
        3,
    )
    product_grad = band_conv(mix_turned, banded(medium_h, block_rows), block_rows)
    grad_blocks = jnp.swapaxes(
        mix_grad.reshape(seq_local, row_count // block_rows, block_rows, group_local, group_size),
        3,
        4,
    )
    filter_part = lag_sums(grad_blocks, windows(product_turned, block_rows, reach), tap_count)
    feature_grad = jnp.stack(
        [query_grad, product_grad * values, product_grad * keys], axis=2
    ).astype(jnp.bfloat16)
    grad_back = from_behind(feature_grad[:, :short_reach], "ctx", -1)
    grad_pad = jnp.concatenate([feature_grad, grad_back], axis=1).astype(jnp.float32)
    grad_projected = adjoint(grad_pad, short_w).astype(jnp.bfloat16)
    short_part = short_sums(
        feature_grad.astype(jnp.float32), padded_input.astype(jnp.float32), short_taps
    )
    filter_total, short_total = lax.psum((filter_part, short_part), ("dp", "ctx"))
    seq_total = seq_local * lax.axis_size("dp")
    length_total = row_count * lax.axis_size("ctx")
    filter_grad = filter_total / math.sqrt(seq_total * length_total * group_size)
    short_grad = short_total / math.sqrt(seq_total * length_total)
    return (block_out, grad_projected, filter_grad, short_grad)


def solution(mesh):
    in_specs = (
        P("dp", "ctx", None, "grp"),
        P(None, None, "grp"),
        P("grp", None),
        P("ctx", "grp"),
        P("dp", "ctx", "grp"),
    )
    out_specs = (
        P("dp", "ctx", "grp"),
        P("dp", "ctx", None, "grp"),
        P("grp", None),
        P(None, None, "grp"),
    )
    return jax.shard_map(shards, mesh=mesh, in_specs=in_specs, out_specs=out_specs, check_vma=False)
```

profile of v0, /device:TPU:1, one launch (start us, length us, event | category | flops | bytes accessed | tf_op | source)
XLA Modules:
  0.0 600.7 jit_solution(14814459723128327061)
XLA Ops:
  8.0 103.6 %all-gather.5.cloned.1.call-done = bf16[4096,1024]{1,0:T(8,128)(2,1)} async-done(((bf16[128,1024]{1,0:T(8,128)(2,1)}), bf16[4096,1024]{1,0:T(8,128)(2,1)}) %all-gather.5.cloned.1.call-update) | async-done | bytes 8388624 | tf_op jit(solution)/shard_map/all_gather | solution.py:127
  111.5 10.1 %fusion.31 = f32[512,4096]{1,0:T(8,128)} fusion(bf16[512,1024]{1,0:T(8,128)(2,1)S(1)} %bitcast.91, bf16[4096,1024]{1,0:T(8,128)(2,1)} %all-gather.5.cloned.1.call-done), kind=kOutput, calls=%fused_computation.57 | convolution fusion | flops 4294967296 | bytes 17825792 | tf_op jit(solution)/shard_map/dot_general | solution.py:131
  122.7 1.7 collective-permute-start
  124.5 4.6 copy.57
  130.0 4.6 maximum_convert_fusion
  134.6 3.6 copy-done.2
  138.3 5.9 multiply_add_fusion
  144.2 58.5 %reduce-scatter.2.cloned.1.call-done = f32[512,1024]{1,0:T(8,128)} async-done(((f32[512,4096]{1,0:T(8,128)}), f32[512,1024]{1,0:T(8,128)}) %reduce-scatter.2.cloned.1.call-update) | async-done | bytes 2097168 | tf_op jit(solution)/shard_map/reduce_scatter | solution.py:137
  202.6 1.7 convert_element_type.49
  204.6 1.8 copy.66
  206.4 2.4 fusion.14
  209.8 1.5 collective-permute-start.2
  211.6 2.6 copy.97
  214.2 2.3 slice.126
  216.5 15.8 %reshape.121 = bf16[64,128,255,1,1]{2,1,0,3,4:T(8,128)(2,1)} reshape(bf16[64,32640]{1,0:T(8,128)(2,1)} %slice.126) | data formatting | bytes 8355840 | tf_op jit(solution)/shard_map/reshape | solution.py:37
  232.3 1.6 pad_maximum_fusion.2
  233.9 1.5 fusion.29
  235.4 2.2 reshape.126
  237.5 2.5 copy.70
  240.1 2.1 reshape.127
  242.2 1.5 copy.95
  243.7 4.1 fusion.20
  247.8 2.4 copy.71
  250.3 3.9 reshape.116
  254.1 5.9 multiply_convert_fusion.1
  260.1 1.0 copy-done.7
  261.1 1.0 slice.119
  262.1 4.8 collective-permute-start.1
  267.3 2.6 copy.96
  269.9 2.3 slice.122
  272.2 16.0 %reshape.120 = bf16[64,128,255,1,1]{2,1,0,3,4:T(8,128)(2,1)} reshape(bf16[64,32640]{1,0:T(8,128)(2,1)} %slice.122) | data formatting | bytes 8355840 | tf_op jit(solution)/shard_map/reshape | solution.py:37
  288.2 1.6 copy.74
  289.8 1.9 copy.65
  291.7 2.6 reshape.117
  294.2 3.3 squeeze.10
  297.5 3.9 fusion.26
  301.4 1.8 pad_maximum_fusion.1
  303.2 1.2 pad_slice_fusion.1
  304.9 1.3 reshape.124
  306.8 1.3 copy-done.5
  308.1 3.7 fusion.17
  311.8 1.1 copy.62
  312.9 2.7 reshape.109
  315.6 3.0 reshape.104
  318.7 6.2 %convolution_bitcast_fusion = f32[64,128,255]{2,1,0:T(8,128)} fusion(bf16[2,2,255,16,64]{2,3,1,0,4:T(8,128)(2,1)} %copy-done.5, bf16[2,2,128,16,64]{2,1,0,3,4:T(2,128)(2,1)S(1)} %copy-done.9), kind=kOutput, calls=%fused_computation.20 | convolution fusion | flops 267386880 | bytes 11493376 | tf_op jit(solution)/shard_map/sbtcg,sbjcg->gtj/dot_general | solution.py:53
  324.9 9.2 %reshape.118 = f32[64,32640]{1,0:T(8,128)} reshape(f32[64,128,255]{2,1,0:T(8,128)} %convolution_bitcast_fusion) | data formatting | bytes 16711680 | tf_op jit(solution)/shard_map/reshape | solution.py:60
  334.1 4.0 pad.16
  338.2 2.5 copy.98
  341.9 2.4 multiply_convert_fusion.2
  344.4 10.9 %fusion = (f32[3,1024]{1,0:T(4,128)S(1)}, f32[3,1024]{1,0:T(4,128)S(1)}, f32[3,1024]{1,0:T(4,128)S(1)}) fusion(f32[2,258,3,1024]{1,3,0,2:T(8,128)} %copy-done.2, bf16[2,256,1,1024]{1,3,0,2:T(8,128)(2,1)S(1)} %copy-done.4, bf16[2,256,1,1024]{1,3,0,2:T(8,128)(2,1)S(1)} %copy-done.3, bf16[2,256,1,1024]{1,3,0,2:T(8,128)(2,1)S(1)} %multiply_convert_fusion.2), kind=kLoop, calls=%fused_computation.3 | loop fusion | flops 14146560 | bytes 22056960 | tf_op jit(solution)/shard_map/reduce_sum | solution.py:93
  356.0 3.4 fusion.13
  359.7 1.4 slice.127
  361.2 1.7 copy.72
  362.9 1.3 collective-permute-start.3
  364.2 3.3 collective-permute-done.3
  367.5 1.7 copy.73
  369.2 2.6 maximum_convert_fusion.1
  371.8 5.8 fusion.4
  377.6 4.6 copy.78
  382.2 145.3 %all-reduce.8.cloned.1.call-done = (f32[64,128]{1,0:T(8,128)}, f32[3,3,1024]{2,0,1:T(4,128)}) async-done(((f32[64,128]{1,0:T(8,128)}, f32[3,3,1024]{2,0,1:T(4,128)}), (f32[64,128]{1,0:T(8,128)}, f32[3,3,1024]{2,0,1:T(4,128)})) %all-reduce.8.cloned.1.call-update) | async-done | bytes 69648 | tf_op jit(solution)/shard_map/psum | solution.py:169
  529.1 1.4 broadcast_multiply_fusion.1
  530.4 46.8 %all-gather.3.cloned.1.call-done = bf16[2,256,4096]{1,2,0:T(8,128)(2,1)} async-done(((bf16[2,256,1024]{1,2,0:T(8,128)(2,1)}), bf16[2,256,4096]{1,2,0:T(8,128)(2,1)}) %all-gather.3.cloned.1.call-update) | async-done | bytes 4194320 | tf_op jit(solution)/shard_map/all_gather | solution.py:122
  577.3 6.5 %copy.63 = bf16[2,256,4096]{2,1,0:T(8,128)(2,1)} copy(bf16[2,256,4096]{1,2,0:T(8,128)(2,1)} %all-gather.3.cloned.1.call-done) | data formatting | bytes 8388608 | tf_op jit(solution)/shard_map/all_gather | solution.py:122
  583.8 10.2 %convolution_convert_fusion = bf16[512,1024]{1,0:T(8,128)(2,1)} fusion(bf16[512,4096]{1,0:T(8,128)(2,1)} %bitcast.102, bf16[4096,1024]{1,0:T(8,128)(2,1)} %all-gather.5.cloned.1.call-done), kind=kOutput, calls=%fused_computation.42 | convolution fusion | flops 4295491584 | bytes 13631488 | tf_op jit(solution)/shard_map/dot_general | solution.py:125
  (53 shorter events, 9.2 us)
Async XLA Ops:
  7.2 104.4 %copy-start = (bf16[2,256,1024]{2,1,0:T(8,128)(2,1)S(1)}, bf16[2,256,1024]{2,1,0:T(8,128)(2,1)}, u32[]{:S(2)}) copy-start(bf16[2,256,1024]{2,1,0:T(8,128)(2,1)} %param.9) | copy-start | bytes 3145732
  7.2 104.3 %all-gather.5.cloned.1.call-start = ((), (), s32[]{:S(2)}) async-start(), calls=%async_computation.2 | async-start | bytes 8650752 | tf_op jit(solution)/shard_map/all_gather | solution.py:127
  7.9 194.7 %reduce-scatter.2.cloned.1.call-start = ((), (), s32[]{:S(2)}) async-start(), calls=%async_computation.3 | async-start | bytes 10485760 | tf_op jit(solution)/shard_map/reduce_scatter | solution.py:137
  121.7 2.8 copy-start.11
  121.7 405.9 %all-reduce.8.cloned.1.call-start = ((), (), s32[]{:S(2)}) async-start(), calls=%async_computation.4 | async-start | bytes 163840 | tf_op jit(solution)/shard_map/psum | solution.py:169
  122.7 6.5 %collective-permute-start = (bf16[2,2,3,1024]{3,1,2,0:T(2,128)(2,1)S(1)}, bf16[2,2,3,1024]{3,1,2,0:T(2,128)(2,1)S(1)}, u32[]{:S(2)}, u32[]{:S(2)}) collective-permute-start(bf16[2,2,3,1024]{3,1,2,0:T(2,128)(2,1)S(1)} %slice.89), channel_id=1, source_target_pairs={{0,4},{4,8},{8,12},{12,16},{16,20},{20,24},{24,28},{28,32},{32,36}... | collective-permute-start | bytes 73736 | tf_op jit(solution)/shard_map/ppermute | solution.py:11
  134.6 3.7 copy-start.2
  206.4 4.8 copy-start.10
  208.9 2.4 copy-start.6
  209.8 22.5 %collective-permute-start.2 = (bf16[2,127,1024]{1,2,0:T(8,128)(2,1)}, bf16[2,127,1024]{1,2,0:T(8,128)(2,1)}, u32[]{:S(2)}, u32[]{:S(2)}) collective-permute-start(bf16[2,127,1024]{1,2,0:T(8,128)(2,1)} %slice.123), channel_id=1, source_target_pairs={{4,0},{8,4},{12,8},{16,12},{20,16},{24,20},{28,24},{32,28},{36,32}... | collective-permute-start | bytes 1560584 | tf_op jit(solution)/shard_map/ppermute | solution.py:11
  260.1 1.0 copy-start.7
  262.1 39.3 %collective-permute-start.1 = (bf16[2,127,1024]{1,2,0:T(8,128)(2,1)}, bf16[2,127,1024]{1,2,0:T(8,128)(2,1)}, u32[]{:S(2)}, u32[]{:S(2)}) collective-permute-start(bf16[2,127,1024]{1,2,0:T(8,128)(2,1)} %slice.119), channel_id=1, source_target_pairs={{0,4},{4,8},{8,12},{12,16},{16,20},{20,24},{24,28},{28,32},{32,36}... | collective-permute-start | bytes 1560584 | tf_op jit(solution)/shard_map/ppermute | solution.py:11
  297.5 3.9 copy-start.8
  306.7 1.3 copy-start.5
  315.6 3.0 copy-start.9
  341.2 3.2 copy-start.3
  341.2 3.2 copy-start.4
  355.9 221.4 %all-gather.3.cloned.1.call-start = ((), (), s32[]{:S(2)}) async-start(), calls=%async_computation.1 | async-start | bytes 5242880 | tf_op jit(solution)/shard_map/all_gather | solution.py:122
  362.9 4.6 collective-permute-start.3
  583.8 10.2 %copy-start.1 = (bf16[2,256,1024]{2,1,0:T(8,128)(2,1)S(1)}, bf16[2,256,1024]{2,1,0:T(8,128)(2,1)}, u32[]{:S(2)}) copy-start(bf16[2,256,1024]{2,1,0:T(8,128)(2,1)} %param.9) | copy-start | bytes 3145732
Sparse Core Ops, SparseCore 0:
  10.6 100.9 all-gather.4
  121.8 80.7 reduce-scatter.1
  356.0 171.5 all-reduce.7
  529.8 47.3 all-gather.2
where the time goes:
time: 607 us; the launch traced here: 601 us
  waiting for transfers between devices  358 us (59%)
  local copies, waits for them, and re-layouts  127 us (21%)
  other arithmetic  56.9 us (9%)
  matrix products  34.4 us (6%)
  between operations  14.3 us (2%)
  starting transfers between devices  9.42 us (2%)
    psum x1, waiting for transfers between devices, shards(): lax.psum((filter_part, short_part), ('dp', 'ctx'))  145 us
    all_gather x1, waiting for transfers between devices, shards(): lax.all_gather(out_w, 'ctx', axis=0, tiled=True)  104 us
    reduce_scatter x1, waiting for transfers between devices, shards(): lax.psum_scatter(input_part, 'grp', scatter_dimension=1, tiled=True)  58.5 us
    all_gather x1, waiting for transfers between devices, shards(): whole_gated = lax.all_gather(gated, 'grp', axis=2, tiled=True)  46.8 us
    reshape x2, local copies, waits for them, and re-layouts, banded(): tiled[:, :block_rows * (line_width - 1)]  31.8 us
    unnamed x34, local copies, waits for them, and re-layouts  25.5 us
  transfers between devices with their start and end apart: 8, of which 5 were waited for; matrix products, arithmetic and copies ran while one was open for 16% of the time, Pallas kernels for 0%

commit v1 on v0

--- a/solution.py
+++ b/solution.py
@@ -124,7 +124,9 @@
     flat_cotangent = grad_out.reshape(seq_local * row_count, chan_local)
     projected_out = jnp.dot(
         flat_gated,
-        lax.all_gather(out_w, "ctx", axis=0, tiled=True),
+        jnp.concatenate(
+            lax.all_to_all(jnp.stack([out_w] * lax.axis_size("ctx")), "ctx", 0, 0), axis=0
+        ),
         preferred_element_type=jnp.float32,
     )
     block_out = projected_out.astype(jnp.bfloat16).reshape(seq_local, row_count, chan_local)

time: 607 us -> 738 us (1.22)
  waiting for transfers between devices: 358 us -> 478 us
  starting transfers between devices: 9.42 us -> 17.5 us
    ppermute x4, waiting for transfers between devices: 3.28 us -> 174 us  [from_behind(): return lax.ppermute(block, axis, route)]
    reduce_scatter x1, waiting for transfers between devices: 58.5 us -> 0.01 us  [shards(): lax.psum_scatter(input_part, 'grp', scatter_dimension=1, tiled=True)]
    psum x1, waiting for transfers between devices: 145 us -> 153 us  [shards(): lax.psum((filter_part, short_part), ('dp', 'ctx'))]
    unnamed x34 -> x40, local copies, waits for them, and re-layouts: 25.5 us -> 26.5 us
  transfers between devices with their start and end apart: 8 -> 9, of which waited for: 5 -> 5; matrix products, arithmetic and copies ran while one was open for 16% -> 26% of each run, Pallas kernels for 0% -> 0%
where the time goes in v1:
time: 738 us; the launch traced here: 730 us
  waiting for transfers between devices  478 us (65%)
  local copies, waits for them, and re-layouts  132 us (18%)
  other arithmetic  55.9 us (8%)
  matrix products  32.1 us (4%)
  starting transfers between devices  17.5 us (2%)
  between operations  14.3 us (2%)
    ppermute x4, waiting for transfers between devices, from_behind(): return lax.ppermute(block, axis, route)  174 us
    psum x1, waiting for transfers between devices, shards(): lax.psum((filter_part, short_part), ('dp', 'ctx'))  153 us
    all_gather x1, waiting for transfers between devices, shards(): lax.all_gather(out_w, 'ctx', axis=0, tiled=True)  104 us
    all_gather x1, waiting for transfers between devices, shards(): whole_gated = lax.all_gather(gated, 'grp', axis=2, tiled=True)  46.8 us
    reshape x2, local copies, waits for them, and re-layouts, banded(): tiled[:, :block_rows * (line_width - 1)]  32 us
    unnamed x40, local copies, waits for them, and re-layouts  26.5 us
  transfers between devices with their start and end apart: 9, of which 5 were waited for; matrix products, arithmetic and copies ran while one was open for 26% of the time, Pallas kernels for 0%

profile of v1, /device:TPU:1, one launch (start us, length us, event | category | flops | bytes accessed | tf_op | source)
XLA Modules:
  0.0 730.0 jit_solution(5225025767518684361)
XLA Ops:
  8.0 103.6 %all-gather.5.cloned.1.call-done = bf16[4096,1024]{1,0:T(8,128)(2,1)} async-done(((bf16[128,1024]{1,0:T(8,128)(2,1)}), bf16[4096,1024]{1,0:T(8,128)(2,1)}) %all-gather.5.cloned.1.call-update) | async-done | bytes 8388624 | tf_op jit(solution)/shard_map/all_gather | solution.py:135
  111.5 10.1 %fusion.31 = f32[512,4096]{1,0:T(8,128)} fusion(bf16[512,1024]{1,0:T(8,128)(2,1)S(1)} %bitcast.92, bf16[4096,1024]{1,0:T(8,128)(2,1)} %all-gather.5.cloned.1.call-done), kind=kOutput, calls=%fused_computation.57 | convolution fusion | flops 4294967296 | bytes 17825792 | tf_op jit(solution)/shard_map/dot_general | solution.py:133
  122.6 4.4 stack.13
  127.0 5.6 all-to-all-start
  133.6 3.1 collective-permute-start
  136.7 4.6 copy.57
  141.4 170.7 %collective-permute-done = bf16[2,2,3,1024]{3,1,2,0:T(2,128)(2,1)S(1)} collective-permute-done((bf16[2,2,3,1024]{3,1,2,0:T(2,128)(2,1)S(1)}, bf16[2,2,3,1024]{3,1,2,0:T(2,128)(2,1)S(1)}, u32[]{:S(2)}, u32[]{:S(2)}) %collective-permute-start) | collective-permute-done | bytes 24608 | tf_op jit(solution)/shard_map/ppermute | solution.py:11
  312.9 3.8 maximum_convert_fusion
  316.7 3.7 copy-done.2
  320.4 5.9 multiply_add_fusion
  326.3 1.7 convert_element_type.49
  328.3 1.8 copy.66
  330.1 2.4 fusion.14
  333.5 1.5 collective-permute-start.2
  335.2 2.6 copy.97
  337.9 2.2 slice.126
  340.1 15.9 %reshape.127 = bf16[64,128,255,1,1]{2,1,0,3,4:T(8,128)(2,1)} reshape(bf16[64,32640]{1,0:T(8,128)(2,1)} %slice.126) | data formatting | bytes 8355840 | tf_op jit(solution)/shard_map/reshape | solution.py:37
  356.0 1.6 pad_maximum_fusion.2
  357.5 1.5 fusion.29
  359.0 2.2 reshape.132
  361.2 2.5 copy.70
  363.7 2.1 reshape.133
  365.9 1.5 copy.95
  367.4 4.1 fusion.20
  371.5 2.4 copy.71
  373.9 3.9 reshape.122
  377.8 5.9 multiply_convert_fusion.1
  383.7 1.0 copy-done.9
  384.7 1.0 slice.119
  385.7 6.0 collective-permute-start.1
  392.1 2.6 copy.96
  394.7 2.2 slice.122
  396.9 16.1 %reshape.126 = bf16[64,128,255,1,1]{2,1,0,3,4:T(8,128)(2,1)} reshape(bf16[64,32640]{1,0:T(8,128)(2,1)} %slice.122) | data formatting | bytes 8355840 | tf_op jit(solution)/shard_map/reshape | solution.py:37
  413.0 1.6 copy.74
  414.6 3.5 reshape.123
  418.1 1.8 copy.65
  419.9 3.4 squeeze.10
  423.4 3.7 fusion.26
  427.1 1.8 pad_maximum_fusion.1
  430.5 1.4 copy-done.3
  431.9 1.6 fusion.17
  433.5 1.1 copy.62
  434.6 2.7 reshape.115
  437.3 3.0 reshape.109
  440.4 6.2 convolution_bitcast_fusion
  446.5 9.3 %reshape.124 = f32[64,32640]{1,0:T(8,128)} reshape(f32[64,128,255]{2,1,0:T(8,128)} %convolution_bitcast_fusion) | data formatting | bytes 16711680 | tf_op jit(solution)/shard_map/reshape | solution.py:60
  455.8 4.0 pad.16
  459.8 2.5 copy.98
  463.6 2.4 multiply_convert_fusion.2
  466.0 10.8 %fusion = (f32[3,1024]{1,0:T(4,128)S(1)}, f32[3,1024]{1,0:T(4,128)S(1)}, f32[3,1024]{1,0:T(4,128)S(1)}) fusion(f32[2,258,3,1024]{1,3,0,2:T(8,128)} %copy-done.2, bf16[2,256,1,1024]{1,3,0,2:T(8,128)(2,1)S(1)} %copy-done.5, bf16[2,256,1,1024]{1,3,0,2:T(8,128)(2,1)S(1)} %copy-done.4, bf16[2,256,1,1024]{1,3,0,2:T(8,128)(2,1)S(1)} %multiply_convert_fusion.2), kind=kLoop, calls=%fused_computation.3 | loop fusion | flops 14146560 | bytes 22056960 | tf_op jit(solution)/shard_map/reduce_sum | solution.py:93
  477.6 3.4 fusion.13
  481.3 1.4 slice.127
  482.7 1.7 copy.72
  484.5 1.3 collective-permute-start.3
  485.8 3.5 collective-permute-done.3
  489.2 1.7 copy.73
  491.0 2.6 maximum_convert_fusion.1
  493.6 5.8 fusion.4
  499.4 4.6 copy.78
  504.0 152.9 %all-reduce.8.cloned.1.call-done = (f32[64,128]{1,0:T(8,128)}, f32[3,3,1024]{2,0,1:T(4,128)}) async-done(((f32[64,128]{1,0:T(8,128)}, f32[3,3,1024]{2,0,1:T(4,128)}), (f32[64,128]{1,0:T(8,128)}, f32[3,3,1024]{2,0,1:T(4,128)})) %all-reduce.8.cloned.1.call-update) | async-done | bytes 69648 | tf_op jit(solution)/shard_map/psum | solution.py:171
  658.4 1.4 broadcast_multiply_fusion.1
  659.8 46.8 %all-gather.3.cloned.1.call-done = bf16[2,256,4096]{1,2,0:T(8,128)(2,1)} async-done(((bf16[2,256,1024]{1,2,0:T(8,128)(2,1)}), bf16[2,256,4096]{1,2,0:T(8,128)(2,1)}) %all-gather.3.cloned.1.call-update) | async-done | bytes 4194320 | tf_op jit(solution)/shard_map/all_gather | solution.py:122
  706.6 6.5 copy.63
  713.1 10.2 %convolution_convert_fusion = bf16[512,1024]{1,0:T(8,128)(2,1)} fusion(bf16[512,4096]{1,0:T(8,128)(2,1)} %bitcast.103, bf16[4096,1024]{1,0:T(8,128)(2,1)} %bitcast.8), kind=kOutput, calls=%fused_computation.42 | convolution fusion | flops 4295491584 | bytes 13631488 | tf_op jit(solution)/shard_map/dot_general | solution.py:125
  (62 shorter events, 10.7 us)
Async XLA Ops:
  7.2 104.4 %copy-start = (bf16[2,256,1024]{2,1,0:T(8,128)(2,1)S(1)}, bf16[2,256,1024]{2,1,0:T(8,128)(2,1)}, u32[]{:S(2)}) copy-start(bf16[2,256,1024]{2,1,0:T(8,128)(2,1)} %param.9) | copy-start | bytes 3145732
  7.2 104.3 %all-gather.5.cloned.1.call-start = ((), (), s32[]{:S(2)}) async-start(), calls=%async_computation.3 | async-start | bytes 8650752 | tf_op jit(solution)/shard_map/all_gather | solution.py:135
  7.9 318.4 %reduce-scatter.2.cloned.1.call-start = ((), (), s32[]{:S(2)}) async-start(), calls=%async_computation.4 | async-start | bytes 10485760 | tf_op jit(solution)/shard_map/reduce_scatter | solution.py:139
  121.6 0.9 copy-start.12
  127.0 9.7 %copy-start.14 = (f32[3,3,1024]{2,1,0:T(4,128)S(1)}, f32[3,3,1024]{2,1,0:T(4,128)}, u32[]{:S(2)}) copy-start(f32[3,3,1024]{2,1,0:T(4,128)} %param.6) | copy-start | bytes 110596
  127.0 586.1 %all-to-all-start = ((bf16[32,128,1024]{2,1,0:T(8,128)(2,1)}), bf16[32,128,1024]{2,1,0:T(8,128)(2,1)}, u32[]{:S(2)}, u32[]{:S(2)}) async-start(bf16[32,128,1024]{2,1,0:T(8,128)(2,1)} %stack.13), calls=%async_computation | async-start | bytes 16777216 | tf_op jit(solution)/shard_map/all_to_all | solution.py:128
  132.6 524.3 %all-reduce.8.cloned.1.call-start = ((), (), s32[]{:S(2)}) async-start(), calls=%async_computation.5 | async-start | bytes 163840 | tf_op jit(solution)/shard_map/psum | solution.py:171
  133.6 178.5 %collective-permute-start = (bf16[2,2,3,1024]{3,1,2,0:T(2,128)(2,1)S(1)}, bf16[2,2,3,1024]{3,1,2,0:T(2,128)(2,1)S(1)}, u32[]{:S(2)}, u32[]{:S(2)}) collective-permute-start(bf16[2,2,3,1024]{3,1,2,0:T(2,128)(2,1)S(1)} %slice.89), channel_id=1, source_target_pairs={{0,4},{4,8},{8,12},{12,16},{16,20},{20,24},{24,28},{28,32},{32,36}... | collective-permute-start | bytes 73736 | tf_op jit(solution)/shard_map/ppermute | solution.py:11
  316.7 3.7 copy-start.2
  330.1 4.8 copy-start.13
  332.6 2.4 copy-start.8
  333.5 22.5 %collective-permute-start.2 = (bf16[2,127,1024]{1,2,0:T(8,128)(2,1)}, bf16[2,127,1024]{1,2,0:T(8,128)(2,1)}, u32[]{:S(2)}, u32[]{:S(2)}) collective-permute-start(bf16[2,127,1024]{1,2,0:T(8,128)(2,1)} %slice.123), channel_id=1, source_target_pairs={{4,0},{8,4},{12,8},{16,12},{20,16},{24,20},{28,24},{32,28},{36,32}... | collective-permute-start | bytes 1560584 | tf_op jit(solution)/shard_map/ppermute | solution.py:11
  383.7 1.0 copy-start.9
  385.7 41.4 %collective-permute-start.1 = (bf16[2,127,1024]{1,2,0:T(8,128)(2,1)}, bf16[2,127,1024]{1,2,0:T(8,128)(2,1)}, u32[]{:S(2)}, u32[]{:S(2)}) collective-permute-start(bf16[2,127,1024]{1,2,0:T(8,128)(2,1)} %slice.119), channel_id=1, source_target_pairs={{0,4},{4,8},{8,12},{12,16},{16,20},{20,24},{24,28},{28,32},{32,36}... | collective-permute-start | bytes 1560584 | tf_op jit(solution)/shard_map/ppermute | solution.py:11
  419.9 3.4 copy-start.7
  419.9 7.2 copy-start.10
  429.7 2.2 copy-start.3
  431.9 1.6 copy-start.6
  434.6 5.7 copy-start.11
  462.3 3.7 copy-start.4
  462.3 3.7 copy-start.5
  477.5 229.1 %all-gather.3.cloned.1.call-start = ((), (), s32[]{:S(2)}) async-start(), calls=%async_computation.2 | async-start | bytes 5242880 | tf_op jit(solution)/shard_map/all_gather | solution.py:122
  484.5 4.8 collective-permute-start.3
  713.1 10.2 %copy-start.1 = (bf16[2,256,1024]{2,1,0:T(8,128)(2,1)S(1)}, bf16[2,256,1024]{2,1,0:T(8,128)(2,1)}, u32[]{:S(2)}) copy-start(bf16[2,256,1024]{2,1,0:T(8,128)(2,1)} %param.9) | copy-start | bytes 3145732
Sparse Core Ops, SparseCore 0:
  10.6 100.9 all-gather.4
  121.8 80.7 reduce-scatter.1
  477.6 179.2 all-reduce.7
  659.2 47.3 all-gather.2
